TPU v7x, 32 devices: a whole 2x2x4 slice. The times are simulated.
32 devices in a mesh: row: 4 (over y, x), col: 8 (over z, core).
Axes of the slice: x: 2, y: 2, z: 4, core: 2. Of those that a mesh axis runs over, the one named last changes fastest.
Arguments:
- amplitudes: bfloat16 [4096, 16384], P('col', 'row'), may hold values from -6 to 6
- integrals: bfloat16 [4096, 16384], P('row', 'col'), may hold values from -0.09375 to 0.09375
- tile_mask: int32 [64, 256], P(None, 'row'), may hold values from 0 to 1, as said below
- occ_energy: float32 [4], replicated, may hold values from -1 to -0.2
- virt_energy: float32 [4096], replicated, may hold values from 0.2 to 1.5
Outputs:
- update: bfloat16 [16384, 16384], P(('row', 'col'))
Inputs may be any that keep to these rules, and one draw needn't show every extreme that they name: `tile_mask`: 0 drops a tile, 1 keeps it; the share of kept tiles differs strongly between groups of (ia) rows.
All inputs are finite; a program needn't handle non-finite values.
Results may differ from a plain program's by a relative error of at most 0.0049.
Values may be sent and summed in bfloat16 or wider, within the bound.
A program may use at most 192 MiB of HBM per device.

v0:
```python
import functools

import jax
import jax.numpy as jnp
from jax import lax
from jax.experimental import pallas as pl
from jax.experimental.pallas import tpu as pltpu
from jax.sharding import PartitionSpec as P

TILE = 64
MESH = pl.DeviceIdType.MESH
VMEM_BYTES = 66_000_000
DIMS = (((0,), (0,)), ((), ()))


def xor(u, v, n):
    total, bit = 0, 1
    while bit < n:
        total = total + (((u // bit) % 2 + (v // bit) % 2) % 2) * bit
        bit *= 2
    return total


def bits_of(n):
    out, bit = [], 1
    while bit < n:
        out.append(bit)
        bit *= 2
    return out


def children(m, parity, n):
    if m == 0:
        return bits_of(n)
    have = [b for b in bits_of(n) if m & b]
    if parity == 0:
        return [b for b in bits_of(n) if b < have[0]]
    return [b for b in bits_of(n) if b > have[-1]]


def after(k, n):
    odd = k % 2 == 1
    up = jnp.where(k + 2 <= n - 1, k + 2, n - 2)
    down = jnp.where(k == 0, 1, k - 2)
    return jnp.where(odd, up, down)


def before(k, n):
    odd = k % 2 == 1
    up = jnp.where(k + 2 <= n - 2, k + 2, n - 1)
    down = jnp.where(k == 1, 0, k - 2)
    return jnp.where(odd, down, up)


def kernel(
    nr, nc, a_ref, b_ref, rg_ref, cg_ref, out, a_full, ib,
    ra, rb, ca, cb, stage, twin,
    s_own, s_fwd, s_part, s_ra, s_rb, s_bc, s_hand, s_rra, s_rrb, s_po, s_out, s_tw,
    q_a, q_g, q_q, q_ra, q_rb, q_out, l_c, l_r,
):
    r = lax.axis_index("row")
    c = lax.axis_index("col")
    n = nc // 2
    k = c // 2
    p = c % 2
    partner = c + 1 - 2 * p
    d, w = a_ref.shape
    e = b_ref.shape[0]
    sub = w // n
    q = sub // 2
    half = n // 2
    depth = d * nc
    nxt, prv = after(k, n), before(k, n)
    low = k < half
    top_skip = (n - 1) - 2 if n > 2 else 0
    bottom_skip = 2
    bits = bits_of(nr)

    barrier = pltpu.get_barrier_semaphore()

    def greet(row, col):
        pl.semaphore_signal(barrier, inc=1, device_id=(row, col), device_id_type=MESH)

    greet(r, partner)
    for m in range(1, nr):
        greet(xor(r, m, nr), c)
        greet(xor(r, m, nr), partner)
    greet(r, (c + 2) % nc)
    greet(r, (c - 2 + nc) % nc)
    for t in range(2):
        greet(r, 2 * nxt + t)
        greet(r, 2 * prv + t)
    pl.semaphore_wait(barrier, 1 + 2 * (nr - 1) + 2 + 4)

    state = {"wait": False}

    def run(cond, body):
        if cond is None:
            body()
        else:
            pl.when(cond)(body)

    def both(*conds):
        total = None
        for x in conds:
            if x is None:
                continue
            total = x if total is None else jnp.logical_and(total, x)
        return total

    def no(x):
        return jnp.logical_not(x)

    def send(src, dst, sem, recv, row, col, cond=None):
        copy = pltpu.make_async_remote_copy(
            src_ref=src, dst_ref=dst, send_sem=sem, recv_sem=recv,
            device_id=(row, col), device_id_type=MESH,
        )
        run(cond, copy.wait_send if state["wait"] else copy.start)

    def local(src, dst, sem, cond=None):
        if not state["wait"]:
            run(cond, pltpu.make_async_copy(src, dst, sem).start)

    def arrived(ref, sem, cond=None):
        if not state["wait"]:
            run(cond, pltpu.make_async_copy(ref, ref, sem).wait)

    def ds(start, size):
        return pl.ds(pl.multiple_of(start, size), size)

    def a_rows(col):
        return ds(col * d, d)

    def b_rows(row):
        return ds(row * e, e)

    def cols(kp):
        return ds(kp * sub, sub)

    def raw(kk, kp, plane):
        direct = jnp.logical_and(kk == r, kp != plane)
        return b_rows(jnp.where(direct, r, nr + kk))

    own = ds(c * q, q)

    def rows_a(src, col, cond):
        for x, b in enumerate(bits):
            send(src, ra.at[b, a_rows(col), :], s_ra.at[col, x], q_ra.at[b, col], xor(r, b, nr), c, cond)

    def b_out(src, kk, kp, cond, mine):
        is_row = both(cond, kp == k)
        for t in range(2):
            part = src.at[:, pl.ds(t * q, q)]
            for x, b in enumerate(bits):
                row = xor(r, b, nr)
                send(part, rb.at[xor(row, kk, nr), b_rows(r), :], s_rb.at[kk, t, x], q_rb.at[b, kk], row, 2 * k + t, is_row)
            dst = rb.at[xor(r, kk, nr), b_rows(r), :]
            local(part, dst, q_rb.at[0, kk], both(is_row, p == t))
            send(part, dst, s_rb.at[kk, t, len(bits)], q_rb.at[0, kk], r, partner, both(is_row, p != t))
        is_col = both(cond, kp != k, kp != prv)
        dst = ib.at[b_rows(r), cols(kp)]
        send(src, dst, s_bc.at[kk, kp], q_q.at[r, kp], kk, c, both(is_col, kk != r))
        send(src, dst, s_bc.at[kk, kp], q_q.at[r, kp], r, partner, both(is_col, kk == r))
        if mine:
            local(src, dst, q_q.at[r, kp], both(is_col, kk == r))

    def blocked(target, kp):
        return jnp.logical_or(
            jnp.logical_and(target == 0, kp == bottom_skip),
            jnp.logical_and(target == n - 1, kp == top_skip),
        )

    def owner(kp):
        return kp // half == p

    def piece(sign, j):
        return n - 1 - j if sign > 0 else j

    def valid(j):
        return jnp.logical_and(j >= 0, j < n)

    def clip(x, top):
        return jnp.clip(x, 0, top)

    def issue_own(sign, j, least=0):
        ok = jnp.logical_and(j >= least, j < n)
        kp = piece(sign, clip(j, n - 1))
        far = k + sign
        ok = both(ok, far >= 0, far < n, no(blocked(far, kp)))
        x = 0 if sign > 0 else 1
        target = clip(c + 2 * sign, nc - 1)
        send(a_ref.at[:, cols(kp)], a_full.at[a_rows(c), cols(kp)], s_own.at[x, 0, kp], q_a.at[c, kp], r, target, ok)
        send(
            b_ref.at[:, cols(kp % half)], ib.at[raw(k, kp, far), cols(kp)], s_own.at[x, 1, kp], q_g.at[k, kp],
            r, target, both(ok, owner(kp)),
        )

    def relay(sign, j, s):
        kp = piece(sign, clip(j, n - 1))
        src = k - sign * s
        here = both(valid(j), src >= 0, src < n, no(blocked(k, kp)))
        kk = clip(src, n - 1)
        far = k + sign
        onward = both(here, far >= 0, far < n, no(blocked(far, kp)))
        x = 0 if sign > 0 else 1
        target = clip(c + 2 * sign, nc - 1)
        col = 2 * kk + p
        a_piece = a_full.at[a_rows(col), cols(kp)]
        arrived(a_piece, q_a.at[col, kp], here)
        send(a_piece, a_piece, s_fwd.at[x, s - 1, 0, kp], q_a.at[col, kp], r, target, onward)
        send(a_piece, a_piece, s_part.at[kk, kp], q_a.at[col, kp], r, partner, both(here, kp != prv))
        rows_a(a_full.at[a_rows(col), own], col, both(here, kp == k))
        mine = both(here, owner(kp))
        b_piece = ib.at[raw(kk, kp, k), cols(kp)]
        arrived(b_piece, q_g.at[kk, kp], mine)
        send(
            b_piece, ib.at[raw(kk, kp, far), cols(kp)], s_fwd.at[x, s - 1, 1, kp], q_g.at[kk, kp],
            r, target, both(onward, owner(kp)),
        )
        b_out(b_piece, kk, kp, mine, False)

    def partner_rows(kk, cond):
        col = 2 * kk + 1 - p
        ref = a_full.at[a_rows(col), cols(k)]
        arrived(ref, q_a.at[col, k], cond)
        rows_a(a_full.at[a_rows(col), own], col, cond)

    def own_part():
        rows_a(a_ref.at[:, own], c, None)

        @pl.loop(0, n)
        def _(kp):
            b_out(b_ref.at[:, cols(kp % half)], k, kp, owner(kp), True)
            part = a_ref.at[:, cols(kp)]
            dst = a_full.at[a_rows(c), cols(kp)]
            send(part, dst, s_part.at[k, kp], q_a.at[c, kp], r, partner, kp != prv)
            local(part, dst, q_a.at[c, kp], kp != prv)

    def slot(tau):
        up = tau + jnp.where(low, 1, 0)
        down = tau + jnp.where(low, 0, 1)
        issue_own(1, up + 1, 1)
        issue_own(-1, down + 1, 1)
        for s in range(1, n):
            relay(1, up, s)
            relay(-1, down, s)
        for s in range(1, n):
            for sign, j in ((1, up), (-1, down)):
                src = k - sign * s
                cond = both(valid(j), src >= 0, src < n, piece(sign, j) == k)
                partner_rows(clip(src, n - 1), cond)

    mirrored = jnp.where(low, k, n - 1 - k)
    ready = jnp.where(mirrored == 0, 0, jnp.maximum(mirrored, n - 2 - mirrored))

    def relay_rows():
        for m in range(nr):
            origin = xor(r, m, nr)

            @pl.loop(0, n)
            def _(kk, m=m, origin=origin):
                for pp in range(2):
                    col = 2 * kk + pp
                    if m:
                        got = ra.at[m, a_rows(col), :]
                        arrived(got, q_ra.at[m, col])
                        for b in children(m, pp, nr):
                            x = bits.index(b)
                            send(got, ra.at[m | b, a_rows(col), :], s_rra.at[col, m, x], q_ra.at[m | b, col], xor(r, b, nr), c)

            @pl.loop(0, half)
            def _(gg, m=m, origin=origin):
                for pg in range(2):
                    g = 2 * gg + pg
                    got = rb.at[xor(r, g, nr), b_rows(origin), :]
                    arrived(got, q_rb.at[m, g])
                    if m:
                        for b in children(m, pg, nr):
                            x = bits.index(b)
                            row = xor(r, b, nr)
                            send(
                                got, rb.at[xor(row, g, nr), b_rows(origin), :], s_rrb.at[g, m, x],
                                q_rb.at[m | b, g], row, c,
                            )
                    send(
                        got, ib.at[b_rows(origin), own], s_po.at[m], q_q.at[origin, k], r, partner, g == r,
                    )

    def hand(kp, cond):
        mine = both(cond, owner(kp))
        for m in range(nr):
            row = xor(r, m, nr)
            ref = ib.at[b_rows(row), cols(kp)]
            if m:
                arrived(ref, q_q.at[row, kp], mine)
                send(ref, ref, s_hand.at[row, kp], q_q.at[row, kp], r, partner, mine)
            else:
                arrived(ref, q_q.at[row, kp], both(mine, k == r))

    def tile_piece(t):
        rank = jnp.where(low, prv, n - 1 - prv)
        base = jnp.where(mirrored < rank, mirrored, mirrored - 1)
        i = jnp.where(t == 0, base, jnp.where(t <= base, t - 1, t))
        i = jnp.where(i >= rank, i + 1, i)
        return jnp.where(low, i, n - 1 - i)

    def tile(t):
        kp = tile_piece(t)
        is_own = kp == k
        for kk in range(n):
            col = 2 * kk + 1 - p
            arrived(a_full.at[a_rows(col), cols(kp)], q_a.at[col, kp], no(is_own))
        arrived(a_full.at[a_rows(c), cols(kp)], q_a.at[c, kp], no(is_own))
        for row in range(nr):
            arrived(ib.at[b_rows(row), cols(kp)], q_q.at[row, kp], both(no(is_own), no(owner(kp))))
            arrived(ib.at[b_rows(row), own], q_q.at[row, k], is_own)

        def load(h):
            where = ds((2 * kp + h) * q, q)
            full = pl.ds(0, depth)
            pltpu.make_async_copy(a_full.at[:, where], ca.at[h], l_c.at[h, 0]).start()
            mine = jnp.logical_and(is_own, p == h)
            run(mine, pltpu.make_async_copy(rb.at[0], cb.at[h], l_c.at[h, 1]).start)
            run(no(mine), pltpu.make_async_copy(ib.at[full, where], cb.at[h], l_c.at[h, 1]).start)

        for h in range(2):
            load(h)

        @pl.loop(0, 2)
        def _(h):
            where = ds((2 * kp + h) * q, q)
            pltpu.make_async_copy(ca.at[h], ca.at[h], l_c.at[h, 0]).wait()
            pltpu.make_async_copy(cb.at[h], cb.at[h], l_c.at[h, 1]).wait()

            @pl.loop(0, nr)
            def _(i):
                m = nr - 1 - i
                row = xor(r, m, nr)
                buf = stage.at[h, m]
                run(t > 0, pltpu.make_async_copy(buf, buf, s_out.at[h, m]).wait)
                total = lax.dot_general(ra[m], cb[h], DIMS, preferred_element_type=jnp.float32)
                total += lax.dot_general(rb[m], ca[h], DIMS, preferred_element_type=jnp.float32)
                total = total / (rg_ref[m] + cg_ref[:, where])
                stage[h, m] = total.astype(stage.dtype)
                dst = out.at[:, ds(r * w + (2 * kp + h) * q, q)]
                remote = pltpu.make_async_remote_copy(
                    src_ref=buf, dst_ref=dst, send_sem=s_out.at[h, m], recv_sem=q_out,
                    device_id=(row, c), device_id_type=MESH,
                )
                run(m > 0, remote.start)
                run(m == 0, pltpu.make_async_copy(buf, dst, s_out.at[h, m]).start)

                @pl.when(kp == nxt)
                def _():
                    twin[h, m] = total.T.astype(twin.dtype)
                    pltpu.make_async_remote_copy(
                        src_ref=twin.at[h, m], dst_ref=out.at[:, ds(row * w + c * q, q)],
                        send_sem=s_tw.at[h, m], recv_sem=q_out,
                        device_id=(r, 2 * kp + h), device_id_type=MESH,
                    ).start()

    end = mirrored == 0

    def start():
        for sign in (1, -1):
            issue_own(sign, jnp.int32(0))
        own_part()
        partner_rows(k, None)

    start()

    @pl.loop(0, n + 1)
    def _(x):
        slot(x - 2)
        pl.when(x - 2 == ready)(relay_rows)

    arrived(a_full.at[a_rows(c), cols(k)], q_a.at[c, k])
    load_own = pltpu.make_async_copy(a_full.at[:, own], ra.at[0], l_r)
    load_own.start()
    load_own.wait()
    hand(tile_piece(1), None)

    @pl.loop(0, n)
    def _(x):
        last = x == jnp.where(end, 2, 1)

        @pl.when(last)
        def _():
            slot(x * 0 + n - 1)
            hand(tile_piece(2), None)

        @pl.when(no(last))
        def _():
            t = jnp.where(x == 0, 0, jnp.where(x > 2, x - 1, 1))
            more = jnp.logical_and(x > 2, x < n - 1)
            hand(tile_piece(jnp.where(more, x, 1)), more)
            tile(t)

    state["wait"] = True
    start()

    @pl.loop(0, n + 2)
    def _(x):
        slot(x - 2)

    relay_rows()

    @pl.loop(1, n - 1)
    def _(t):
        hand(tile_piece(t), None)

    @pl.loop(0, 2)
    def _(h):
        @pl.loop(0, nr)
        def _(m):
            pltpu.make_async_copy(stage.at[h, m], stage.at[h, m], s_out.at[h, m]).wait()
            pltpu.make_async_copy(twin.at[h, m], twin.at[h, m], s_tw.at[h, m]).wait()

    landed = out.at[:, pl.ds(0, (nr - 1) * (n - 1) * sub + nr * sub)]
    pltpu.make_async_copy(landed, landed, q_out).wait()


def fused(nr, nc, a, b, row_gap, col_gap):
    d, w = a.shape
    e = b.shape[0]
    n = nc // 2
    depth = d * nc
    q = w // nc
    nb = len(bits_of(nr))
    dma = pltpu.SemaphoreType.DMA
    hbm = pl.BlockSpec(memory_space=pl.ANY)
    vmem = pl.BlockSpec(memory_space=pltpu.VMEM)
    shapes = [(q, nr * w), (depth, w), ((nr + n) * e, w)]
    block = pltpu.VMEM((nr, depth, q), a.dtype)
    pair = pltpu.VMEM((2, depth, q), a.dtype)
    tiles = pltpu.VMEM((2, nr, q, q), a.dtype)
    return pl.pallas_call(
        functools.partial(kernel, nr, nc),
        out_shape=[jax.ShapeDtypeStruct(s, a.dtype) for s in shapes],
        in_specs=[hbm, hbm, vmem, vmem],
        out_specs=[hbm] * 3,
        scratch_shapes=[
            block, block, pair, pair, tiles, tiles,
            dma((2, 2, n)), dma((2, n - 1, 2, n)), dma((n, n)), dma((nc, nb)), dma((n, 2, nb + 1)),
            dma((n, n)), dma((nr, n)), dma((nc, nr, nb)), dma((n, nr, nb)), dma((nr,)), dma((2, nr)), dma((2, nr)),
            dma((nc, n)), dma((n, n)), dma((nr, n)), dma((nr, nc)), dma((nr, n)), dma, dma((2, 2)), dma,
        ],
        compiler_params=pltpu.CompilerParams(
            collective_id=0, has_side_effects=True, vmem_limit_bytes=VMEM_BYTES,
        ),
    )(a, b, row_gap, col_gap)


def local(amplitudes, integrals, tile_mask, occ_energy, virt_energy):
    nr = lax.axis_size("row")
    nc = lax.axis_size("col")
    r = lax.axis_index("row")
    c = lax.axis_index("col")
    depth, width = amplitudes.shape
    tile_rows = depth // TILE
    tile_cols = width // TILE
    own_mask = lax.dynamic_slice_in_dim(tile_mask, c * tile_rows, tile_rows, 0)
    keep_tiles = own_mask.astype(jnp.bfloat16)
    keep = jnp.broadcast_to(keep_tiles[:, :, None], (tile_rows, tile_cols, TILE)).reshape(tile_rows, 1, width)
    masked = (amplitudes.reshape(tile_rows, TILE, width) * keep).reshape(depth, width)
    q = width // nc
    pair_gap = (virt_energy[None, :] - occ_energy[:, None]).reshape(-1)
    col_gap = lax.dynamic_slice_in_dim(pair_gap, r * width, width, 0)[None, :]
    row_gap = jnp.stack([lax.dynamic_slice_in_dim(pair_gap, (r ^ m) * width + c * q, q, 0) for m in range(nr)])
    return fused(nr, nc, masked, integrals, row_gap[:, :, None], col_gap)[0]


def solution(mesh):
    return jax.shard_map(
        local,
        mesh=mesh,
        in_specs=(P("col", "row"), P("row", "col"), P(None, "row"), P(), P()),
        out_specs=P(("row", "col"), None),
        check_vma=False,
    )
```

profile of v0, /device:TPU:4, one launch (start us, length us, event | category | flops | bytes accessed | tf_op | source)
XLA Modules:
  0.0 811.8 jit_solution(3973253080588251422)
XLA Ops:
  0.0 0.7 dynamic-slice_convert_fusion
  0.7 0.8 subtract_bitcast_fusion
  1.5 0.1 fusion
  1.6 0.6 dynamic_slice.23
  2.2 0.1 broadcast_in_dim.6
  2.4 0.2 mul.36
  2.5 1.3 copy.6.rg_ref
  3.9 4.5 bitcast_multiply_fusion.a_ref
  8.4 789.6 %shard_map.55 = (bf16[512,16384]{1,0:T(8,128)(2,1)}, bf16[4096,4096]{1,0:T(8,128)(2,1)}, bf16[8192,4096]{1,0:T(8,128)(2,1)}) custom-call(bf16[512,4096]{1,0:T(8,128)(2,1)} %bitcast_multiply_fusion.a_ref, bf16[1024,2048]{1,0:T(8,128)(2,1)} %b_ref.1, f32[4,512,1]{2,1,0:T(8,128)} %copy.6.rg_ref, f32[1,4096]{1,0:T(1,128)} %bitcast.14), custom_call_target="tpu_custom_call" | custom-call | tf_op jit(solution)/shard_map/pallas_call | solution.py:438
  798.0 13.8 %copy.9 = bf16[512,16384]{1,0:T(8,128)(2,1)} copy(bf16[512,16384]{1,0:T(8,128)(2,1)} %get-tuple-element.6) | data formatting | bytes 33554432
  (2 shorter events, 0.0 us)
where the time goes:
time: 812 us
  Pallas kernels  790 us (97%)
  local copies, waits for them, and re-layouts  16.1 us (2%)
    pallas_call x1, Pallas kernels, fused(): pl.pallas_call(functools.partial(kernel, nr, nc), out_shape=[jax.ShapeDty...  790 us

commit v1 on v0

--- a/solution.py
+++ b/solution.py
@@ -55,8 +55,8 @@
 def kernel(
     nr, nc, a_ref, b_ref, rg_ref, cg_ref, out, a_full, ib,
     ra, rb, ca, cb, stage, twin,
-    s_own, s_fwd, s_part, s_ra, s_rb, s_bc, s_hand, s_rra, s_rrb, s_po, s_out, s_tw,
-    q_a, q_g, q_q, q_ra, q_rb, q_out, l_c, l_r,
+    s_tr, s_own, s_fwd, s_part, s_ra, s_rb, s_bc, s_hand, s_rra, s_rrb, s_po, s_out, s_tw,
+    q_tr, q_a, q_g, q_q, q_ra, q_rb, q_out, l_c, l_r,
 ):
     r = lax.axis_index("row")
     c = lax.axis_index("col")
@@ -66,14 +66,18 @@
     partner = c + 1 - 2 * p
     d, w = a_ref.shape
     e = b_ref.shape[0]
+    eh = e // 2
     sub = w // n
     q = sub // 2
     half = n // 2
     depth = d * nc
-    nxt, prv = after(k, n), before(k, n)
+    nxt, prv = before(k, n), after(k, n)
     low = k < half
-    top_skip = (n - 1) - 2 if n > 2 else 0
-    bottom_skip = 2
+    top_skip, bottom_skip = n - 2, 1
+    mirrored = jnp.where(low, k, n - 1 - k)
+    first = jnp.where(mirrored == 0, -1, 0)
+    early = jnp.where(mirrored == 0, -1, n - 2 - mirrored)
+    late = jnp.where(mirrored == 0, 0, mirrored + 1)
     bits = bits_of(nr)
 
     barrier = pltpu.get_barrier_semaphore()
@@ -138,9 +142,12 @@
     def cols(kp):
         return ds(kp * sub, sub)
 
+    def h_rows(row, pp):
+        return ds((2 * row + pp) * eh, eh)
+
     def raw(kk, kp, plane):
         direct = jnp.logical_and(kk == r, kp != plane)
-        return b_rows(jnp.where(direct, r, nr + kk))
+        return ds(jnp.where(direct, 2 * r + p, 2 * nr + kk) * eh, eh)
 
     own = ds(c * q, q)
 
@@ -148,22 +155,37 @@
         for x, b in enumerate(bits):
             send(src, ra.at[b, a_rows(col), :], s_ra.at[col, x], q_ra.at[b, col], xor(r, b, nr), c, cond)
 
-    def b_out(src, kk, kp, cond, mine):
+    def b_out(src, kk, kp, cond):
         is_row = both(cond, kp == k)
         for t in range(2):
             part = src.at[:, pl.ds(t * q, q)]
             for x, b in enumerate(bits):
                 row = xor(r, b, nr)
-                send(part, rb.at[xor(row, kk, nr), b_rows(r), :], s_rb.at[kk, t, x], q_rb.at[b, kk], row, 2 * k + t, is_row)
-            dst = rb.at[xor(r, kk, nr), b_rows(r), :]
-            local(part, dst, q_rb.at[0, kk], both(is_row, p == t))
-            send(part, dst, s_rb.at[kk, t, len(bits)], q_rb.at[0, kk], r, partner, both(is_row, p != t))
-        is_col = both(cond, kp != k, kp != prv)
-        dst = ib.at[b_rows(r), cols(kp)]
-        send(src, dst, s_bc.at[kk, kp], q_q.at[r, kp], kk, c, both(is_col, kk != r))
-        send(src, dst, s_bc.at[kk, kp], q_q.at[r, kp], r, partner, both(is_col, kk == r))
-        if mine:
-            local(src, dst, q_q.at[r, kp], both(is_col, kk == r))
+                send(
+                    part, rb.at[xor(row, kk, nr), h_rows(r, p), :], s_rb.at[kk, t, x], q_rb.at[b, kk, p],
+                    row, 2 * k + t, is_row,
+                )
+            dst = rb.at[xor(r, kk, nr), h_rows(r, p), :]
+            local(part, dst, q_rb.at[0, kk, p], both(is_row, p == t))
+            send(part, dst, s_rb.at[kk, t, len(bits)], q_rb.at[0, kk, p], r, partner, both(is_row, p != t))
+
+    def spread(src, kk, kp, cond):
+        ok = both(cond, kp != k, kp != prv)
+        dst = ib.at[h_rows(r, p), cols(kp)]
+        send(src, dst, s_bc.at[kk, kp], q_q.at[r, kp, p], kk, c, both(ok, kk != r))
+        send(src, dst, s_bc.at[kk, kp], q_q.at[r, kp, p], r, partner, both(ok, kk == r))
+
+    def mine_of(kp):
+        return (
+            (b_ref.at[ds(p * eh, eh), cols(kp % half)], owner(kp)),
+            (ib.at[ds((2 * nr + k) * eh, eh), cols(kp)], no(owner(kp))),
+        )
+
+    def trade():
+        other = 1 - p
+        dst = ib.at[ds((2 * nr + k) * eh, eh), ds(p * (w // 2), w // 2)]
+        send(b_ref.at[ds(other * eh, eh), :], dst, s_tr, q_tr, r, partner)
+        arrived(dst, q_tr)
 
     def blocked(target, kp):
         return jnp.logical_or(
@@ -177,48 +199,73 @@
     def piece(sign, j):
         return n - 1 - j if sign > 0 else j
 
+    def swap(j):
+        return jnp.where(j == 1, 2, jnp.where(j == 2, 1, j))
+
+    def edge(sign):
+        return 0 if sign > 0 else n - 1
+
     def valid(j):
         return jnp.logical_and(j >= 0, j < n)
 
     def clip(x, top):
         return jnp.clip(x, 0, top)
 
-    def issue_own(sign, j, least=0):
-        ok = jnp.logical_and(j >= least, j < n)
-        kp = piece(sign, clip(j, n - 1))
+    def issue_own(sign, j, when=None):
+        ok = both(valid(j), when)
+        kp = piece(sign, jnp.where(k == edge(sign), swap(clip(j, n - 1)), clip(j, n - 1)))
         far = k + sign
         ok = both(ok, far >= 0, far < n, no(blocked(far, kp)))
         x = 0 if sign > 0 else 1
         target = clip(c + 2 * sign, nc - 1)
         send(a_ref.at[:, cols(kp)], a_full.at[a_rows(c), cols(kp)], s_own.at[x, 0, kp], q_a.at[c, kp], r, target, ok)
-        send(
-            b_ref.at[:, cols(kp % half)], ib.at[raw(k, kp, far), cols(kp)], s_own.at[x, 1, kp], q_g.at[k, kp],
-            r, target, both(ok, owner(kp)),
-        )
-
-    def relay(sign, j, s):
-        kp = piece(sign, clip(j, n - 1))
+        for src, cond in mine_of(kp):
+            send(
+                src, ib.at[raw(k, kp, far), cols(kp)], s_own.at[x, 1, kp], q_g.at[k, kp],
+                r, target, both(ok, cond),
+            )
+
+    def order(sign, j, s, src):
+        j = clip(j, n - 1)
+        return piece(sign, jnp.where(src == edge(sign), swap(j), j) if s == 1 else j)
+
+    def relay(sign, j, s, tau):
         src = k - sign * s
+        kp = order(sign, j, s, src)
         here = both(valid(j), src >= 0, src < n, no(blocked(k, kp)))
         kk = clip(src, n - 1)
         far = k + sign
-        onward = both(here, far >= 0, far < n, no(blocked(far, kp)))
         x = 0 if sign > 0 else 1
         target = clip(c + 2 * sign, nc - 1)
         col = 2 * kk + p
+
+        def onward(which, kp, cond):
+            ok = both(cond, valid(j), src >= 0, src < n, far >= 0, far < n, no(blocked(far, kp)))
+            if which == 0:
+                ref = a_full.at[a_rows(col), cols(kp)]
+                send(ref, ref, s_fwd.at[x, s - 1, 0, kp], q_a.at[col, kp], r, target, ok)
+            else:
+                send(
+                    ib.at[raw(kk, kp, k), cols(kp)], ib.at[raw(kk, kp, far), cols(kp)],
+                    s_fwd.at[x, s - 1, 1, kp], q_g.at[kk, kp], r, target, ok,
+                )
+
+        held = both(src == edge(sign), j == 1) if s == 1 else None
+        freed = both(src == edge(sign), j == 2)
         a_piece = a_full.at[a_rows(col), cols(kp)]
         arrived(a_piece, q_a.at[col, kp], here)
-        send(a_piece, a_piece, s_fwd.at[x, s - 1, 0, kp], q_a.at[col, kp], r, target, onward)
+        onward(0, kp, no(held) if s == 1 else None)
         send(a_piece, a_piece, s_part.at[kk, kp], q_a.at[col, kp], r, partner, both(here, kp != prv))
         rows_a(a_full.at[a_rows(col), own], col, both(here, kp == k))
-        mine = both(here, owner(kp))
         b_piece = ib.at[raw(kk, kp, k), cols(kp)]
-        arrived(b_piece, q_g.at[kk, kp], mine)
-        send(
-            b_piece, ib.at[raw(kk, kp, far), cols(kp)], s_fwd.at[x, s - 1, 1, kp], q_g.at[kk, kp],
-            r, target, both(onward, owner(kp)),
-        )
-        b_out(b_piece, kk, kp, mine, False)
+        arrived(b_piece, q_g.at[kk, kp], here)
+        onward(1, kp, no(held) if s == 1 else None)
+        if s == 1:
+            onward(0, order(sign, 1, 1, src), freed)
+            onward(1, order(sign, 1, 1, src), freed)
+        issue_own(sign, j + 1, both(valid(j), src == edge(sign)))
+        b_out(b_piece, kk, kp, here)
+        spread(b_piece, kk, kp, both(here, tau > late))
 
     def partner_rows(kk, cond):
         col = 2 * kk + 1 - p
@@ -231,7 +278,9 @@
 
         @pl.loop(0, n)
         def _(kp):
-            b_out(b_ref.at[:, cols(kp % half)], k, kp, owner(kp), True)
+            for src, cond in mine_of(kp):
+                b_out(src, k, kp, cond)
+                local(src, ib.at[h_rows(r, p), cols(kp)], q_q.at[r, kp, p], both(cond, k == r, kp != k, kp != prv))
             part = a_ref.at[:, cols(kp)]
             dst = a_full.at[a_rows(c), cols(kp)]
             send(part, dst, s_part.at[k, kp], q_a.at[c, kp], r, partner, kp != prv)
@@ -240,63 +289,81 @@
     def slot(tau):
         up = tau + jnp.where(low, 1, 0)
         down = tau + jnp.where(low, 0, 1)
-        issue_own(1, up + 1, 1)
-        issue_own(-1, down + 1, 1)
+        issue_own(1, up + 1, both(valid(up), k == 0))
+        issue_own(-1, down + 1, both(valid(down), k == n - 1))
         for s in range(1, n):
-            relay(1, up, s)
-            relay(-1, down, s)
+            relay(1, up, s, tau)
+            relay(-1, down, s, tau)
         for s in range(1, n):
             for sign, j in ((1, up), (-1, down)):
                 src = k - sign * s
-                cond = both(valid(j), src >= 0, src < n, piece(sign, j) == k)
+                cond = both(valid(j), src >= 0, src < n, order(sign, j, s, src) == k)
                 partner_rows(clip(src, n - 1), cond)
 
-    mirrored = jnp.where(low, k, n - 1 - k)
-    ready = jnp.where(mirrored == 0, 0, jnp.maximum(mirrored, n - 2 - mirrored))
-
-    def relay_rows():
-        for m in range(nr):
-            origin = xor(r, m, nr)
-
-            @pl.loop(0, n)
-            def _(kk, m=m, origin=origin):
-                for pp in range(2):
-                    col = 2 * kk + pp
-                    if m:
-                        got = ra.at[m, a_rows(col), :]
-                        arrived(got, q_ra.at[m, col])
-                        for b in children(m, pp, nr):
-                            x = bits.index(b)
-                            send(got, ra.at[m | b, a_rows(col), :], s_rra.at[col, m, x], q_ra.at[m | b, col], xor(r, b, nr), c)
-
-            @pl.loop(0, half)
-            def _(gg, m=m, origin=origin):
-                for pg in range(2):
-                    g = 2 * gg + pg
-                    got = rb.at[xor(r, g, nr), b_rows(origin), :]
-                    arrived(got, q_rb.at[m, g])
-                    if m:
-                        for b in children(m, pg, nr):
-                            x = bits.index(b)
-                            row = xor(r, b, nr)
-                            send(
-                                got, rb.at[xor(row, g, nr), b_rows(origin), :], s_rrb.at[g, m, x],
-                                q_rb.at[m | b, g], row, c,
-                            )
+    def pass_rows(kk, m, cond):
+        origin = xor(r, m, nr)
+        for pp in range(2):
+            if m:
+                col = 2 * kk + pp
+                got = ra.at[m, a_rows(col), :]
+                arrived(got, q_ra.at[m, col], cond)
+                for b in children(m, pp, nr):
+                    x = bits.index(b)
                     send(
-                        got, ib.at[b_rows(origin), own], s_po.at[m], q_q.at[origin, k], r, partner, g == r,
+                        got, ra.at[m | b, a_rows(col), :], s_rra.at[col, m, x], q_ra.at[m | b, col],
+                        xor(r, b, nr), c, cond,
                     )
+            got = rb.at[xor(r, kk, nr), h_rows(origin, pp), :]
+            arrived(got, q_rb.at[m, kk, pp], cond)
+            if m:
+                for b in children(m, pp, nr):
+                    x = bits.index(b)
+                    row = xor(r, b, nr)
+                    send(
+                        got, rb.at[xor(row, kk, nr), h_rows(origin, pp), :], s_rrb.at[kk, m, pp, x],
+                        q_rb.at[m | b, kk, pp], row, c, cond,
+                    )
+            dst = ib.at[h_rows(origin, pp), own]
+            send(got, dst, s_po.at[m, pp], q_q.at[origin, k, pp], r, partner, both(cond, kk == r))
+
+    def pass_direct(tau):
+        @pl.loop(0, n)
+        def _(kk):
+            near = jnp.where((kk < k) == low, early, late)
+            when = jnp.where(kk == k, first, near)
+            for m in bits:
+                pass_rows(kk, m, tau == when)
+
+    def pass_rest():
+        @pl.loop(0, n)
+        def _(kk):
+            for m in range(nr):
+                if m not in bits:
+                    pass_rows(kk, m, None)
+
+    def spread_all(tau):
+        @pl.loop(0, n)
+        def _(kp):
+            for m in [*range(1, nr), 0]:
+                kk = xor(r, m, nr)
+                up = jnp.where(jnp.logical_and(kk == 0, k == 1), swap(n - 1 - kp), n - 1 - kp)
+                down = jnp.where(jnp.logical_and(kk == n - 1, k == n - 2), swap(kp), kp)
+                came = jnp.where(kk < k, up - jnp.where(low, 1, 0), down - jnp.where(low, 0, 1))
+                ok = both(tau == late, no(blocked(k, kp)))
+                for src, cond in mine_of(kp):
+                    spread(src, kk, kp, both(ok, kk == k, cond))
+                there = ib.at[raw(kk, kp, k), cols(kp)]
+                spread(there, kk, kp, both(ok, kk != k, came <= late))
 
     def hand(kp, cond):
-        mine = both(cond, owner(kp))
         for m in range(nr):
             row = xor(r, m, nr)
-            ref = ib.at[b_rows(row), cols(kp)]
+            ref = ib.at[h_rows(row, p), cols(kp)]
             if m:
-                arrived(ref, q_q.at[row, kp], mine)
-                send(ref, ref, s_hand.at[row, kp], q_q.at[row, kp], r, partner, mine)
+                arrived(ref, q_q.at[row, kp, p], cond)
+                send(ref, ref, s_hand.at[row, kp], q_q.at[row, kp, p], r, partner, cond)
             else:
-                arrived(ref, q_q.at[row, kp], both(mine, k == r))
+                arrived(ref, q_q.at[row, kp, p], both(cond, k == r))
 
     def tile_piece(t):
         rank = jnp.where(low, prv, n - 1 - prv)
@@ -313,8 +380,9 @@
             arrived(a_full.at[a_rows(col), cols(kp)], q_a.at[col, kp], no(is_own))
         arrived(a_full.at[a_rows(c), cols(kp)], q_a.at[c, kp], no(is_own))
         for row in range(nr):
-            arrived(ib.at[b_rows(row), cols(kp)], q_q.at[row, kp], both(no(is_own), no(owner(kp))))
-            arrived(ib.at[b_rows(row), own], q_q.at[row, k], is_own)
+            arrived(ib.at[h_rows(row, 1 - p), cols(kp)], q_q.at[row, kp, 1 - p], no(is_own))
+            for pp in range(2):
+                arrived(ib.at[h_rows(row, pp), own], q_q.at[row, k, pp], is_own)
 
         def load(h):
             where = ds((2 * kp + h) * q, q)
@@ -363,6 +431,7 @@
     end = mirrored == 0
 
     def start():
+        trade()
         for sign in (1, -1):
             issue_own(sign, jnp.int32(0))
         own_part()
@@ -370,31 +439,30 @@
 
     start()
 
-    @pl.loop(0, n + 1)
+    @pl.loop(0, jnp.where(end, n + 1, n + 2))
     def _(x):
         slot(x - 2)
-        pl.when(x - 2 == ready)(relay_rows)
-
+        pass_direct(x - 2)
+        spread_all(x - 2)
+
+    pass_rest()
     arrived(a_full.at[a_rows(c), cols(k)], q_a.at[c, k])
     load_own = pltpu.make_async_copy(a_full.at[:, own], ra.at[0], l_r)
     load_own.start()
     load_own.wait()
-    hand(tile_piece(1), None)
-
-    @pl.loop(0, n)
+
+    @pl.loop(0, jnp.where(end, n, n - 1))
     def _(x):
-        last = x == jnp.where(end, 2, 1)
+        last = jnp.logical_and(end, x == 2)
 
         @pl.when(last)
         def _():
             slot(x * 0 + n - 1)
-            hand(tile_piece(2), None)
 
         @pl.when(no(last))
         def _():
-            t = jnp.where(x == 0, 0, jnp.where(x > 2, x - 1, 1))
-            more = jnp.logical_and(x > 2, x < n - 1)
-            hand(tile_piece(jnp.where(more, x, 1)), more)
+            t = jnp.where(jnp.logical_and(end, x > 2), x - 1, x)
+            hand(tile_piece(t), t > 0)
             tile(t)
 
     state["wait"] = True
@@ -403,8 +471,10 @@
     @pl.loop(0, n + 2)
     def _(x):
         slot(x - 2)
-
-    relay_rows()
+        pass_direct(x - 2)
+        spread_all(x - 2)
+
+    pass_rest()
 
     @pl.loop(1, n - 1)
     def _(t):
@@ -431,7 +501,7 @@
     dma = pltpu.SemaphoreType.DMA
     hbm = pl.BlockSpec(memory_space=pl.ANY)
     vmem = pl.BlockSpec(memory_space=pltpu.VMEM)
-    shapes = [(q, nr * w), (depth, w), ((nr + n) * e, w)]
+    shapes = [(q, nr * w), (depth, w), (nr * e + n * e // 2, w)]
     block = pltpu.VMEM((nr, depth, q), a.dtype)
     pair = pltpu.VMEM((2, depth, q), a.dtype)
     tiles = pltpu.VMEM((2, nr, q, q), a.dtype)
@@ -442,9 +512,9 @@
         out_specs=[hbm] * 3,
         scratch_shapes=[
             block, block, pair, pair, tiles, tiles,
-            dma((2, 2, n)), dma((2, n - 1, 2, n)), dma((n, n)), dma((nc, nb)), dma((n, 2, nb + 1)),
-            dma((n, n)), dma((nr, n)), dma((nc, nr, nb)), dma((n, nr, nb)), dma((nr,)), dma((2, nr)), dma((2, nr)),
-            dma((nc, n)), dma((n, n)), dma((nr, n)), dma((nr, nc)), dma((nr, n)), dma, dma((2, 2)), dma,
+            dma, dma((2, 2, n)), dma((2, n - 1, 2, n)), dma((n, n)), dma((nc, nb)), dma((n, 2, nb + 1)),
+            dma((n, n)), dma((nr, n)), dma((nc, nr, nb)), dma((n, nr, 2, nb)), dma((nr, 2)), dma((2, nr)), dma((2, nr)),
+            dma, dma((nc, n)), dma((n, n)), dma((nr, n, 2)), dma((nr, nc)), dma((nr, n, 2)), dma, dma((2, 2)), dma,
         ],
         compiler_params=pltpu.CompilerParams(
             collective_id=0, has_side_effects=True, vmem_limit_bytes=VMEM_BYTES,

time: 812 us -> 679 us (0.84)
  Pallas kernels: 790 us -> 654 us
    pallas_call x1, Pallas kernels: 790 us -> 654 us  [fused(): pl.pallas_call(functools.partial(kernel, nr, nc), out_shape=[jax.ShapeDty...]
where the time goes in v1:
time: 679 us; the launch traced here: 677 us
  Pallas kernels  654 us (96%)
  local copies, waits for them, and re-layouts  16.1 us (2%)
    pallas_call x1, Pallas kernels, fused(): pl.pallas_call(functools.partial(kernel, nr, nc), out_shape=[jax.ShapeDty...  654 us
    unnamed x2, local copies, waits for them, and re-layouts  13.8 us

profile of v1, /device:TPU:4, one launch (start us, length us, event | category | flops | bytes accessed | tf_op | source)
XLA Modules:
  0.0 676.7 jit_solution(4840698356013660886)
XLA Ops:
  0.0 0.7 dynamic-slice_convert_fusion
  0.7 0.8 subtract_bitcast_fusion
  1.5 0.1 fusion
  1.6 0.6 dynamic_slice.23
  2.2 0.1 broadcast_in_dim.6
  2.4 0.2 mul.36
  2.6 1.3 copy.6.rg_ref
  3.9 4.5 bitcast_multiply_fusion.a_ref
  8.4 654.5 %shard_map.55 = (bf16[512,16384]{1,0:T(8,128)(2,1)}, bf16[4096,4096]{1,0:T(8,128)(2,1)}, bf16[6144,4096]{1,0:T(8,128)(2,1)}) custom-call(bf16[512,4096]{1,0:T(8,128)(2,1)} %bitcast_multiply_fusion.a_ref, bf16[1024,2048]{1,0:T(8,128)(2,1)} %b_ref.1, f32[4,512,1]{2,1,0:T(8,128)} %copy.6.rg_ref, f32[1,4096]{1,0:T(1,128)} %bitcast.14), custom_call_target="tpu_custom_call" | custom-call | tf_op jit(solution)/shard_map/pallas_call | solution.py:508
  662.9 13.8 %copy.9 = bf16[512,16384]{1,0:T(8,128)(2,1)} copy(bf16[512,16384]{1,0:T(8,128)(2,1)} %get-tuple-element.6) | data formatting | bytes 33554432
  (2 shorter events, 0.0 us)

commit v2 on v1

--- a/solution.py
+++ b/solution.py
@@ -197,13 +197,13 @@
         return kp // half == p
 
     def piece(sign, j):
-        return n - 1 - j if sign > 0 else j
+        return jnp.where(sign > 0, n - 1 - j, j)
 
     def swap(j):
         return jnp.where(j == 1, 2, jnp.where(j == 2, 1, j))
 
     def edge(sign):
-        return 0 if sign > 0 else n - 1
+        return jnp.where(sign > 0, 0, n - 1)
 
     def valid(j):
         return jnp.logical_and(j >= 0, j < n)
@@ -216,7 +216,7 @@
         kp = piece(sign, jnp.where(k == edge(sign), swap(clip(j, n - 1)), clip(j, n - 1)))
         far = k + sign
         ok = both(ok, far >= 0, far < n, no(blocked(far, kp)))
-        x = 0 if sign > 0 else 1
+        x = jnp.where(sign > 0, 0, 1)
         target = clip(c + 2 * sign, nc - 1)
         send(a_ref.at[:, cols(kp)], a_full.at[a_rows(c), cols(kp)], s_own.at[x, 0, kp], q_a.at[c, kp], r, target, ok)
         for src, cond in mine_of(kp):
@@ -229,13 +229,13 @@
         j = clip(j, n - 1)
         return piece(sign, jnp.where(src == edge(sign), swap(j), j) if s == 1 else j)
 
-    def relay(sign, j, s, tau):
-        src = k - sign * s
+    def relay(sign, j, s, tau, go):
+        src = jnp.where(go, k - sign * s, -1)
         kp = order(sign, j, s, src)
         here = both(valid(j), src >= 0, src < n, no(blocked(k, kp)))
         kk = clip(src, n - 1)
         far = k + sign
-        x = 0 if sign > 0 else 1
+        x = jnp.where(sign > 0, 0, 1)
         target = clip(c + 2 * sign, nc - 1)
         col = 2 * kk + p
 
@@ -260,10 +260,14 @@
         b_piece = ib.at[raw(kk, kp, k), cols(kp)]
         arrived(b_piece, q_g.at[kk, kp], here)
         onward(1, kp, no(held) if s == 1 else None)
+        last = both(valid(j), src == edge(sign))
         if s == 1:
+            issue_own(sign, 2, freed)
             onward(0, order(sign, 1, 1, src), freed)
             onward(1, order(sign, 1, 1, src), freed)
-        issue_own(sign, j + 1, both(valid(j), src == edge(sign)))
+            issue_own(sign, j + 1, both(last, j != 1))
+        else:
+            issue_own(sign, j + jnp.where(far == edge(-sign), 2, 1), last)
         b_out(b_piece, kk, kp, here)
         spread(b_piece, kk, kp, both(here, tau > late))
 
@@ -286,17 +290,18 @@
             send(part, dst, s_part.at[k, kp], q_a.at[c, kp], r, partner, kp != prv)
             local(part, dst, q_a.at[c, kp], kp != prv)
 
-    def slot(tau):
-        up = tau + jnp.where(low, 1, 0)
-        down = tau + jnp.where(low, 0, 1)
-        issue_own(1, up + 1, both(valid(up), k == 0))
-        issue_own(-1, down + 1, both(valid(down), k == n - 1))
+    def slot(tau, lo=1, hi=None):
+        lag = jnp.where(low, -1, 1)
+        ways = ((lag, tau), (-lag, tau + 1))
+        hi = n - 1 if hi is None else hi
         for s in range(1, n):
-            relay(1, up, s, tau)
-            relay(-1, down, s, tau)
+            go = jnp.logical_and(s >= lo, s <= hi)
+            for sign, j in ways:
+                relay(sign, j, s, tau, go)
         for s in range(1, n):
-            for sign, j in ((1, up), (-1, down)):
-                src = k - sign * s
+            go = jnp.logical_and(s >= lo, s <= hi)
+            for sign, j in ways:
+                src = jnp.where(go, k - sign * s, -1)
                 cond = both(valid(j), src >= 0, src < n, order(sign, j, s, src) == k)
                 partner_rows(clip(src, n - 1), cond)
 
@@ -433,17 +438,25 @@
     def start():
         trade()
         for sign in (1, -1):
-            issue_own(sign, jnp.int32(0))
+            for j in range(n):
+                issue_own(jnp.int32(sign), jnp.int32(j), None if j == 0 else k == edge(sign))
         own_part()
         partner_rows(k, None)
 
     start()
 
-    @pl.loop(0, jnp.where(end, n + 1, n + 2))
+    @pl.loop(0, n + 2)
     def _(x):
-        slot(x - 2)
-        pass_direct(x - 2)
-        spread_all(x - 2)
+        i = x - 3
+        ahead = jnp.logical_and(end, i >= 0)
+        final = i == n - 2
+        tau = jnp.where(ahead, jnp.where(final, 2, i + 2), x - 2)
+        lo = jnp.where(jnp.logical_and(ahead, final), 2, 1)
+        hi = jnp.where(jnp.logical_and(final, no(end)), 1, jnp.where(jnp.logical_and(ahead, no(final)), 1, n - 1))
+        slot(tau, lo, hi)
+        fresh = jnp.where(ahead, n, tau)
+        pass_direct(fresh)
+        spread_all(fresh)
 
     pass_rest()
     arrived(a_full.at[a_rows(c), cols(k)], q_a.at[c, k])
@@ -453,15 +466,13 @@
 
     @pl.loop(0, jnp.where(end, n, n - 1))
     def _(x):
-        last = jnp.logical_and(end, x == 2)
-
-        @pl.when(last)
+        @pl.when(jnp.logical_or(jnp.logical_and(end, jnp.logical_and(x > 1, x < n - 1)), jnp.logical_and(no(end), x == 1)))
         def _():
-            slot(x * 0 + n - 1)
-
-        @pl.when(no(last))
+            slot(jnp.where(end, x + 1, n - 1), 2)
+
+        @pl.when(no(jnp.logical_and(end, x == 1)))
         def _():
-            t = jnp.where(jnp.logical_and(end, x > 2), x - 1, x)
+            t = jnp.where(jnp.logical_and(end, x > 1), x - 1, x)
             hand(tile_piece(t), t > 0)
             tile(t)
 

time: 679 us -> 584 us (0.86)
  Pallas kernels: 654 us -> 554 us
    pallas_call x1, Pallas kernels: 654 us -> 554 us  [fused(): pl.pallas_call(functools.partial(kernel, nr, nc), out_shape=[jax.ShapeDty...]
where the time goes in v2:
time: 584 us; the launch traced here: 576 us
  Pallas kernels  554 us (95%)
  local copies, waits for them, and re-layouts  16.1 us (3%)
  other arithmetic  6.02 us (1%)
    pallas_call x1, Pallas kernels, fused(): pl.pallas_call(functools.partial(kernel, nr, nc), out_shape=[jax.ShapeDty...  554 us
    unnamed x2, local copies, waits for them, and re-layouts  13.8 us

profile of v2, /device:TPU:4, one launch (start us, length us, event | category | flops | bytes accessed | tf_op | source)
XLA Modules:
  0.0 576.1 jit_solution(4558765387790017175)
XLA Ops:
  0.0 0.7 dynamic-slice_convert_fusion
  0.7 0.8 subtract_bitcast_fusion
  1.5 0.1 fusion
  1.6 0.6 dynamic_slice.23
  2.2 0.1 broadcast_in_dim.6
  2.4 0.2 mul.36
  2.6 1.3 copy.6.rg_ref
  3.9 4.5 bitcast_multiply_fusion.a_ref
  8.4 553.9 %shard_map.55 = (bf16[512,16384]{1,0:T(8,128)(2,1)}, bf16[4096,4096]{1,0:T(8,128)(2,1)}, bf16[6144,4096]{1,0:T(8,128)(2,1)}) custom-call(bf16[512,4096]{1,0:T(8,128)(2,1)} %bitcast_multiply_fusion.a_ref, bf16[1024,2048]{1,0:T(8,128)(2,1)} %b_ref.1, f32[4,512,1]{2,1,0:T(8,128)} %copy.6.rg_ref, f32[1,4096]{1,0:T(1,128)} %bitcast.14), custom_call_target="tpu_custom_call" | custom-call | tf_op jit(solution)/shard_map/pallas_call | solution.py:519
  562.3 13.8 %copy.9 = bf16[512,16384]{1,0:T(8,128)(2,1)} copy(bf16[512,16384]{1,0:T(8,128)(2,1)} %get-tuple-element.6) | data formatting | bytes 33554432
  (2 shorter events, 0.0 us)

commit v3 on v2

--- a/solution.py
+++ b/solution.py
@@ -75,7 +75,8 @@
     low = k < half
     top_skip, bottom_skip = n - 2, 1
     mirrored = jnp.where(low, k, n - 1 - k)
-    first = jnp.where(mirrored == 0, -1, 0)
+    end = mirrored == 0
+    first = -1
     early = jnp.where(mirrored == 0, -1, n - 2 - mirrored)
     late = jnp.where(mirrored == 0, 0, mirrored + 1)
     bits = bits_of(nr)
@@ -229,7 +230,7 @@
         j = clip(j, n - 1)
         return piece(sign, jnp.where(src == edge(sign), swap(j), j) if s == 1 else j)
 
-    def relay(sign, j, s, tau, go):
+    def relay(sign, j, s, tau, go, hold):
         src = jnp.where(go, k - sign * s, -1)
         kp = order(sign, j, s, src)
         here = both(valid(j), src >= 0, src < n, no(blocked(k, kp)))
@@ -269,7 +270,7 @@
         else:
             issue_own(sign, j + jnp.where(far == edge(-sign), 2, 1), last)
         b_out(b_piece, kk, kp, here)
-        spread(b_piece, kk, kp, both(here, tau > late))
+        spread(b_piece, kk, kp, both(here, tau > late, None if hold is None else no(hold)))
 
     def partner_rows(kk, cond):
         col = 2 * kk + 1 - p
@@ -290,14 +291,14 @@
             send(part, dst, s_part.at[k, kp], q_a.at[c, kp], r, partner, kp != prv)
             local(part, dst, q_a.at[c, kp], kp != prv)
 
-    def slot(tau, lo=1, hi=None):
+    def slot(tau, lo=1, hi=None, hold=None):
         lag = jnp.where(low, -1, 1)
         ways = ((lag, tau), (-lag, tau + 1))
         hi = n - 1 if hi is None else hi
         for s in range(1, n):
             go = jnp.logical_and(s >= lo, s <= hi)
             for sign, j in ways:
-                relay(sign, j, s, tau, go)
+                relay(sign, j, s, tau, go, hold)
         for s in range(1, n):
             go = jnp.logical_and(s >= lo, s <= hi)
             for sign, j in ways:
@@ -334,7 +335,9 @@
     def pass_direct(tau):
         @pl.loop(0, n)
         def _(kk):
-            near = jnp.where((kk < k) == low, early, late)
+            away = jnp.abs(kk - k)
+            lag = jnp.where(away == 1, mirrored, late)
+            near = jnp.where((kk < k) == low, early, lag)
             when = jnp.where(kk == k, first, near)
             for m in bits:
                 pass_rows(kk, m, tau == when)
@@ -346,7 +349,7 @@
                 if m not in bits:
                     pass_rows(kk, m, None)
 
-    def spread_all(tau):
+    def spread_all(go, held=False):
         @pl.loop(0, n)
         def _(kp):
             for m in [*range(1, nr), 0]:
@@ -354,11 +357,15 @@
                 up = jnp.where(jnp.logical_and(kk == 0, k == 1), swap(n - 1 - kp), n - 1 - kp)
                 down = jnp.where(jnp.logical_and(kk == n - 1, k == n - 2), swap(kp), kp)
                 came = jnp.where(kk < k, up - jnp.where(low, 1, 0), down - jnp.where(low, 0, 1))
-                ok = both(tau == late, no(blocked(k, kp)))
+                ok = both(go, no(blocked(k, kp)))
                 for src, cond in mine_of(kp):
                     spread(src, kk, kp, both(ok, kk == k, cond))
                 there = ib.at[raw(kk, kp, k), cols(kp)]
-                spread(there, kk, kp, both(ok, kk != k, came <= late))
+                ready = came <= late
+                if held:
+                    away = jnp.abs(kk - k)
+                    ready = jnp.logical_or(ready, jnp.logical_or(away == 1, jnp.logical_and(away == 2, came == 2)))
+                spread(there, kk, kp, both(ok, kk != k, ready))
 
     def hand(kp, cond):
         for m in range(nr):
@@ -402,6 +409,7 @@
 
         @pl.loop(0, 2)
         def _(h):
+            pl.when(both(end, h == 1, t > 0, t + 2 < n))(functools.partial(slot, t + 2, 3))
             where = ds((2 * kp + h) * q, q)
             pltpu.make_async_copy(ca.at[h], ca.at[h], l_c.at[h, 0]).wait()
             pltpu.make_async_copy(cb.at[h], cb.at[h], l_c.at[h, 1]).wait()
@@ -433,7 +441,6 @@
                         device_id=(r, 2 * kp + h), device_id_type=MESH,
                     ).start()
 
-    end = mirrored == 0
 
     def start():
         trade()
@@ -445,30 +452,38 @@
 
     start()
 
-    @pl.loop(0, n + 2)
+    @pl.loop(0, n + 3)
     def _(x):
         i = x - 3
         ahead = jnp.logical_and(end, i >= 0)
         final = i == n - 2
-        tau = jnp.where(ahead, jnp.where(final, 2, i + 2), x - 2)
-        lo = jnp.where(jnp.logical_and(ahead, final), 2, 1)
-        hi = jnp.where(jnp.logical_and(final, no(end)), 1, jnp.where(jnp.logical_and(ahead, no(final)), 1, n - 1))
-        slot(tau, lo, hi)
-        fresh = jnp.where(ahead, n, tau)
-        pass_direct(fresh)
-        spread_all(fresh)
+        first_part = jnp.logical_and(no(end), x - 2 == late)
+        second_part = jnp.logical_and(no(end), x - 2 == late + 1)
+        plain = jnp.where(jnp.logical_or(end, x - 2 <= late), x - 2, x - 3)
+        closing = jnp.logical_and(no(end), x == n + 2)
+        tau = jnp.where(ahead, jnp.where(final, 2, i + 2), plain)
+        lo = jnp.where(jnp.logical_or(jnp.logical_and(ahead, final), second_part), 2, 1)
+        top = jnp.where(jnp.logical_or(first_part, closing), 1, n - 1)
+        hi = jnp.where(ahead, jnp.where(i > n - 2, 0, lo), top)
+        slot(tau, lo, hi, end)
+        pass_direct(jnp.where(jnp.logical_or(ahead, second_part), n, plain))
+        spread_all(both(no(end), no(first_part), plain == late))
 
     pass_rest()
     arrived(a_full.at[a_rows(c), cols(k)], q_a.at[c, k])
     load_own = pltpu.make_async_copy(a_full.at[:, own], ra.at[0], l_r)
     load_own.start()
     load_own.wait()
+    spread_all(end, True)
 
     @pl.loop(0, jnp.where(end, n, n - 1))
     def _(x):
-        @pl.when(jnp.logical_or(jnp.logical_and(end, jnp.logical_and(x > 1, x < n - 1)), jnp.logical_and(no(end), x == 1)))
+        @pl.when(jnp.logical_or(jnp.logical_and(end, jnp.logical_and(x > 0, x < n - 1)), jnp.logical_and(no(end), x == 1)))
         def _():
-            slot(jnp.where(end, x + 1, n - 1), 2)
+            slot(
+                jnp.where(end, x + 1, n - 1), jnp.where(jnp.logical_and(end, x == 1), 3, 2),
+                jnp.where(jnp.logical_and(end, x > 1), 2, n - 1),
+            )
 
         @pl.when(no(jnp.logical_and(end, x == 1)))
         def _():
@@ -483,7 +498,7 @@
     def _(x):
         slot(x - 2)
         pass_direct(x - 2)
-        spread_all(x - 2)
+        spread_all(x - 2 == late)
 
     pass_rest()
 

time: 584 us -> 591 us (1.012)
  the two profiles are of different devices: /device:TPU:4 before, /device:TPU:26 now
where the time goes in v3:
time: 591 us; the launch traced here: 590 us
  Pallas kernels  568 us (96%)
  local copies, waits for them, and re-layouts  16.1 us (3%)
  other arithmetic  6.02 us (1%)
    pallas_call x1, Pallas kernels, fused(): pl.pallas_call(functools.partial(kernel, nr, nc), out_shape=[jax.ShapeDty...  568 us
    unnamed x2, local copies, waits for them, and re-layouts  13.8 us

profile of v3, /device:TPU:26, one launch (start us, length us, event | category | flops | bytes accessed | tf_op | source)
XLA Modules:
  0.0 590.2 jit_solution(4257267744965286980)
XLA Ops:
  0.0 0.7 dynamic-slice_convert_fusion
  0.7 0.8 subtract_bitcast_fusion
  1.5 0.1 fusion
  1.6 0.6 dynamic_slice.23
  2.2 0.1 broadcast_in_dim.6
  2.4 0.2 mul.36
  2.6 1.3 copy.6.rg_ref
  3.9 4.5 bitcast_multiply_fusion.a_ref
  8.4 568.0 %shard_map.55 = (bf16[512,16384]{1,0:T(8,128)(2,1)}, bf16[4096,4096]{1,0:T(8,128)(2,1)}, bf16[6144,4096]{1,0:T(8,128)(2,1)}) custom-call(bf16[512,4096]{1,0:T(8,128)(2,1)} %bitcast_multiply_fusion.a_ref, bf16[1024,2048]{1,0:T(8,128)(2,1)} %b_ref.1, f32[4,512,1]{2,1,0:T(8,128)} %copy.6.rg_ref, f32[1,4096]{1,0:T(1,128)} %bitcast.14), custom_call_target="tpu_custom_call" | custom-call | tf_op jit(solution)/shard_map/pallas_call | solution.py:534
  576.4 13.8 %copy.9 = bf16[512,16384]{1,0:T(8,128)(2,1)} copy(bf16[512,16384]{1,0:T(8,128)(2,1)} %get-tuple-element.6) | data formatting | bytes 33554432
  (2 shorter events, 0.0 us)
